TPU v7x, 256 devices: a whole 4x4x8 slice. The times are simulated.
256 devices in a mesh: dp: 8 (over x, core), ctx: 32 (over y, z).
Axes of the slice: x: 4, y: 4, z: 8, core: 2. Of those that a mesh axis runs over, the one named last changes fastest.
Arguments:
- tokens: bfloat16 [32768, 4096], P(('dp', 'ctx')), parts along dimension 0, may hold values from -6 to 6
- pick_flags: int32 [32768], P(('dp', 'ctx')), parts along dimension 0, may hold values from 0 to 1, as said below
- gate_scales: bfloat16 [32768], P(('dp', 'ctx')), parts along dimension 0, may hold values from 0.099609375 to 1
- attn_gain: float32 [4096], replicated, may hold values from 0.4 to 1.6
- query_weight: bfloat16 [4096, 4096], P(None, 'ctx')
- key_weight: bfloat16 [4096, 1024], P(None, 'ctx')
- value_matrix: bfloat16 [4096, 1024], P(None, 'ctx'), may hold values from -0.09375 to 0.09375
- output_weight: bfloat16 [4096, 4096], P('ctx'), may hold values from -0.09375 to 0.09375
- ffn_gain: float32 [4096], replicated, may hold values from 0.25 to 1.75
- gate_weight: bfloat16 [4096, 11264], P(None, 'ctx'), may hold values from -0.09375 to 0.09375
- up_weight: bfloat16 [4096, 11264], P(None, 'ctx'), may hold values from -0.09375 to 0.09375
- down_weight: bfloat16 [11264, 4096], P('ctx'), may hold values from -0.0546875 to 0.0546875
Outputs:
- block_out: bfloat16 [32768, 4096], P(('dp', 'ctx')), parts along dimension 0
There are 8 independent parts, one for each index of `dp`. A program takes and returns all parts, laid end to end along the dimension named above; an argument that names none is the same for every part. Nothing has to cross between parts.
Inputs may be any that keep to these rules, and one draw needn't show every extreme that they name: `pick_flags`: each device's 128 tokens hold at most 32 picks, the first device exactly 32; each document holds exactly 512 picks; a device may hold none.
All inputs are finite; a program needn't handle non-finite values.
Results may differ from a plain program's by a relative error of at most 0.01.
Values may be sent and summed in bfloat16 or wider, within the bound.
A program may use at most 128 MiB of HBM per device.

v0:
```python
import jax
import jax.numpy as jnp
from jax import lax
from jax.sharding import PartitionSpec as P

QUERY_HEADS = 32
KEY_VALUE_HEADS = 8
HEAD_SIZE = 128
PICK_DEV = 16
MOST = 32
norm_eps = 1e-05
rope_base = 500000.0


def rms_scale(matrix, gain_vec):
    mean_square = jnp.mean(matrix * matrix, axis=-1, keepdims=True)
    return matrix * lax.rsqrt(mean_square + norm_eps) * gain_vec


def apply_rotary(values, token_positions):
    half_dim = values.shape[-1] // 2
    frequency = rope_base ** (-(jnp.arange(half_dim, dtype=jnp.float32) * 2.0) / values.shape[-1])
    angles = token_positions.astype(jnp.float32)[:, None] * frequency[None, :]
    cosine = jnp.cos(angles)
    sine_part = jnp.sin(angles)
    lower_half = values[..., :half_dim]
    upper_half = values[..., half_dim:]
    return jnp.concatenate(
        (
            lower_half * cosine - upper_half * sine_part,
            upper_half * cosine + lower_half * sine_part,
        ),
        axis=-1,
    )


def reduce_scatter_rows(partial, ctx_size):
    rows, width = partial.shape
    pieces = lax.all_to_all(
        partial.reshape(ctx_size, rows // ctx_size, width), "ctx", 0, 0, tiled=True
    )
    return jnp.sum(pieces.astype(jnp.float32), axis=0)


def body(
    tokens,
    pick_flags,
    gate_scales,
    attn_gain,
    query_weight,
    key_weight,
    value_matrix,
    output_weight,
    ffn_gain,
    gate_weight,
    up_weight,
    down_weight,
):
    tok_local, width = tokens.shape
    ctx_size = lax.axis_size("ctx")
    my_index = lax.axis_index("ctx")
    picked_count = PICK_DEV * ctx_size
    half_pick = PICK_DEV // 2
    half_cycle = ctx_size // 2
    slot_of = jnp.cumsum(pick_flags) - 1
    token_ids = jnp.arange(tok_local, dtype=jnp.int32)
    slot_match = (jnp.arange(MOST, dtype=jnp.int32)[:, None] == slot_of[None, :]) & (
        pick_flags[None, :] == 1
    )
    chosen = jnp.sum(jnp.where(slot_match, token_ids[None, :], 0), axis=1)
    filled = jnp.any(slot_match, axis=1)
    local_index = jnp.where(filled, chosen, -1)
    padded_rows = jnp.where(filled[:, None], tokens[chosen], jnp.zeros((), jnp.bfloat16))
    padded_gate = jnp.where(filled, gate_scales[chosen], jnp.zeros((), jnp.bfloat16))
    lane = jnp.arange(128, dtype=jnp.int32)[None, :]
    extra = jnp.where(
        lane == 0,
        local_index.astype(jnp.bfloat16)[:, None],
        jnp.where(lane == 1, padded_gate[:, None], jnp.zeros((), jnp.bfloat16)),
    )
    packed = jnp.concatenate((padded_rows, extra), axis=1)
    all_packed = lax.all_gather(packed, "ctx", axis=0, tiled=True)
    all_rows = all_packed[:, :width]
    all_index = all_packed[:, width].astype(jnp.int32)
    all_gate = all_packed[:, width + 1]
    counts = jnp.sum((all_index >= 0).reshape(ctx_size, MOST).astype(jnp.int32), axis=1)
    run_ends = jnp.cumsum(counts)
    run_starts = run_ends - counts
    order_ids = jnp.arange(picked_count, dtype=jnp.int32)
    owner_of = order_ids // PICK_DEV
    within = order_ids % PICK_DEV
    low_part = within < half_pick
    rank_block = jnp.where(low_part, owner_of, (owner_of + half_cycle) % ctx_size)
    rank_inner = jnp.where(low_part, 2 * within, 2 * (within - half_pick) + 1)
    rank_ids = rank_block * PICK_DEV + rank_inner
    source = jnp.sum((run_ends[None, :] <= rank_ids[:, None]).astype(jnp.int32), axis=1)
    flat_row = source * MOST + rank_ids - run_starts[source]
    picked_rows = all_rows[flat_row]
    scales = all_gate[flat_row].astype(jnp.float32)
    token_positions = source * tok_local + all_index[flat_row]
    normalized_rows = rms_scale(picked_rows.astype(jnp.float32), attn_gain).astype(jnp.bfloat16)
    queries = jnp.dot(normalized_rows, query_weight, preferred_element_type=jnp.float32)
    queries = apply_rotary(queries, token_positions).astype(jnp.bfloat16)
    kv_weight = jnp.concatenate((key_weight, value_matrix), axis=1)
    kv_local = jnp.einsum(
        "pd,dc->cp", normalized_rows, kv_weight, preferred_element_type=jnp.float32
    ).astype(jnp.bfloat16)
    comps = key_weight.shape[1] // KEY_VALUE_HEADS
    query_group_width = QUERY_HEADS // KEY_VALUE_HEADS
    by_head = jnp.transpose(kv_local.reshape(2, comps, KEY_VALUE_HEADS, picked_count), (2, 0, 1, 3))
    send = jnp.repeat(by_head, query_group_width, axis=0)
    got = lax.all_to_all(send, "ctx", 0, 0, tiled=True)
    key_cols = got[:, 0].reshape(ctx_size * comps, picked_count)
    value_cols = got[:, 1].reshape(ctx_size * comps, picked_count)
    keys_here = apply_rotary(key_cols.T.astype(jnp.float32), token_positions).astype(jnp.bfloat16)
    values_here = value_cols.T
    scores = jnp.dot(queries, keys_here.T, preferred_element_type=jnp.float32) / jnp.sqrt(
        jnp.float32(HEAD_SIZE)
    )
    allowed = token_positions[None, :] <= token_positions[:, None]
    scores = jnp.where(allowed, scores, -jnp.inf)
    row_max = jnp.max(scores, axis=1, keepdims=True)
    exp_terms = jnp.exp(scores - row_max)
    prob_bf = (exp_terms / jnp.sum(exp_terms, axis=1, keepdims=True)).astype(jnp.bfloat16)
    head_out = jnp.dot(prob_bf, values_here, preferred_element_type=jnp.float32).astype(
        jnp.bfloat16
    )
    own_start = my_index * PICK_DEV
    own_rows = lax.dynamic_slice_in_dim(picked_rows, own_start, PICK_DEV, 0).astype(jnp.float32)
    attn_own = reduce_scatter_rows(
        jnp.dot(head_out, output_weight, preferred_element_type=jnp.float32).astype(jnp.bfloat16),
        ctx_size,
    )
    mixed_own = own_rows + attn_own
    normed_own = rms_scale(mixed_own, ffn_gain).astype(jnp.bfloat16)
    normed_ffn = lax.all_gather(normed_own, "ctx", axis=0, tiled=True)
    gate_proj = jnp.dot(normed_ffn, gate_weight, preferred_element_type=jnp.float32)
    up_proj = jnp.dot(normed_ffn, up_weight, preferred_element_type=jnp.float32)
    hidden = (jax.nn.silu(gate_proj) * up_proj).astype(jnp.bfloat16)
    ffn_own = reduce_scatter_rows(
        jnp.dot(hidden, down_weight, preferred_element_type=jnp.float32).astype(jnp.bfloat16),
        ctx_size,
    )
    scale_own = lax.dynamic_slice_in_dim(scales, own_start, PICK_DEV, 0)
    final_own = (own_rows + scale_own[:, None] * (attn_own + ffn_own)).astype(jnp.bfloat16)
    final_all = lax.all_gather(final_own, "ctx", axis=0, tiled=True)
    my_start = run_starts[my_index]
    rank_here = jnp.clip(my_start + slot_of, 0, picked_count - 1)
    inner_here = rank_here % PICK_DEV
    odd_here = inner_here % 2
    owner_here = (rank_here // PICK_DEV + odd_here * half_cycle) % ctx_size
    take_rows = owner_here * PICK_DEV + inner_here // 2 + odd_here * half_pick
    return jnp.where(pick_flags[:, None] == 1, final_all[take_rows], tokens)


def solution(mesh):
    in_specs = (
        P(("dp", "ctx"), None),
        P(("dp", "ctx")),
        P(("dp", "ctx")),
        P(),
        P(None, "ctx"),
        P(None, "ctx"),
        P(None, "ctx"),
        P("ctx", None),
        P(),
        P(None, "ctx"),
        P(None, "ctx"),
        P("ctx", None),
    )
    out_specs = P(("dp", "ctx"), None)
    return jax.shard_map(body, mesh=mesh, in_specs=in_specs, out_specs=out_specs, check_vma=False)
```

profile of v0, /device:TPU:2, one launch (start us, length us, event | category | flops | bytes accessed | tf_op | source)
XLA Modules:
  0.0 593.0 jit_solution(4322541667487675454)
XLA Ops:
  6.5 0.8 broadcast_compare_fusion
  7.4 0.8 copy.22
  8.2 0.2 reduce-window.13
  8.3 0.1 add_reduce_fusion
  8.5 0.1 fusion.55
  8.6 0.1 select_reduce_fusion
  8.7 1.4 gather_fusion.1
  10.1 2.3 gather_fusion
  12.4 0.1 broadcast_select_fusion.1
  12.5 0.1 select_select_fusion
  12.6 0.7 pad_maximum_fusion
  13.3 0.0 all-gather.4.cloned.1.call-update
  13.4 102.9 %all-gather.4.cloned.1.call-done = bf16[1024,4224]{1,0:T(8,128)(2,1)} async-done(((bf16[32,4224]{1,0:T(8,128)(2,1)}), bf16[1024,4224]{1,0:T(8,128)(2,1)}) %all-gather.4.cloned.1.call-update) | async-done | bytes 8650768 | tf_op jit(solution)/shard_map/all_gather | solution.py:82
  116.3 1.3 convert_reduce_fusion.2
  117.6 0.1 reshape.501
  117.7 0.1 reduce_sum.78
  117.8 0.1 copy.23
  117.9 0.1 reduce-window.14
  118.0 0.1 reduce.2
  118.1 0.1 convert_reduce_fusion.4
  118.2 0.7 fusion.77
  118.9 0.7 fusion.76
  119.6 4.4 compare_select_fusion.5
  124.0 0.2 compare_reduce_fusion.24
  124.1 15.2 %select_select_fusion.1 = s32[512]{0:T(512)S(1)} fusion(pred[512]{0:T(512)(128)(4,1)S(1)} %get-tuple-element.31, pred[512]{0:T(512)(128)(4,1)S(1)} %get-tuple-element.30, pred[512]{0:T(512)(128)(4,1)S(1)} %get-tuple-element.29, pred[512]{0:T(512)(128)(4,1)S(1)} %get-tuple-element.28, pred[512]{0:T(512)(128)(4,1)S(1)} %get-tuple-element.27, ...), kind=kLoop, calls=%fused_computation.170 | loop fusion | flops 12800 | bytes 16996 | tf_op jit(solution)/shard_map/gather | solution.py:97
  139.4 7.7 %slice.81 = bf16[1024,4096]{1,0:T(8,128)(2,1)} slice(bf16[1024,4224]{1,0:T(8,128)(2,1)} %all-gather.4.cloned.1.call-done), slice={[0:1024], [0:4096]} | slice | bytes 16777216 | tf_op jit(solution)/shard_map/slice | solution.py:83
  147.2 13.0 %gather_fusion.2 = bf16[512,4096]{1,0:T(8,128)(2,1)} fusion(bf16[1024,4096]{1,0:T(8,128)(2,1)} %slice.81, s32[1024]{0:T(1024)S(1)} %pad_clamp_fusion.1), kind=kCustom, calls=%fused_computation.2 | custom fusion | bytes 8390656 | tf_op jit(solution)/shard_map/gather | solution.py:98
  160.2 2.3 gather_fusion.4
  162.5 3.2 fusion
  165.8 0.2 copy-done.1
  165.9 2.5 fusion.9
  168.5 0.8 broadcast_in_dim.126
  169.3 5.8 all-to-all-start
  175.1 4.8 fusion.7
  179.9 6.9 %all-to-all-done = bf16[32,2,4,512]{3,2,1,0:T(4,128)(2,1)S(1)} async-done(((bf16[32,2,4,512]{3,2,1,0:T(4,128)(2,1)}), bf16[32,2,4,512]{3,2,1,0:T(4,128)(2,1)S(1)}, u32[]{:S(2)}, u32[]{:S(2)}) %all-to-all-start) | async-done | bytes 262176 | tf_op jit(solution)/shard_map/all_to_all | solution.py:112
  186.8 0.7 slice_convert_fusion
  187.5 0.1 reshape.503
  187.6 0.9 reshape_squeeze.4
  188.6 1.6 fusion.35
  190.1 0.4 fusion.78
  190.5 1.0 copy-done.2
  191.5 0.2 fusion.12
  191.7 5.1 convolution_convert_fusion
  196.8 4.9 all-to-all-start.1
  201.7 0.0 all-gather.6.cloned.1.call-start
  201.8 95.8 %all-to-all-done.1 = bf16[32,16,4096]{2,1,0:T(8,128)(2,1)} async-done(((bf16[32,16,4096]{2,1,0:T(8,128)(2,1)}), bf16[32,16,4096]{2,1,0:T(8,128)(2,1)}, u32[]{:S(2)}, u32[]{:S(2)}) %all-to-all-start.1) | async-done | bytes 4194336 | tf_op jit(solution)/shard_map/all_to_all | solution.py:39
  297.5 2.9 convert_reduce_fusion.1
  300.4 1.1 multiply_reduce_fusion
  301.5 1.7 multiply_convert_fusion
  303.2 77.5 %all-gather.6.cloned.1.call-done = bf16[512,4096]{1,0:T(8,128)(2,1)} async-done(((bf16[16,4096]{1,0:T(8,128)(2,1)}), bf16[512,4096]{1,0:T(8,128)(2,1)}) %all-gather.6.cloned.1.call-update) | async-done | bytes 4194320 | tf_op jit(solution)/shard_map/all_gather | solution.py:136
  380.7 5.6 fusion.79
  386.3 9.2 %convolution_convert_fusion.1 = bf16[512,4096]{1,0:T(8,128)(2,1)} fusion(bf16[352,4096]{1,0:T(8,128)(2,1)S(1)} %copy-done, bf16[512,4096]{1,0:T(8,128)(2,1)} %all-gather.6.cloned.1.call-done, bf16[4096,352]{0,1:T(8,128)(2,1)} %param.22, f32[512,352]{0,1:T(8,128)} %fusion.79), kind=kOutput, calls=%fused_computation.14 | convolution fusion | flops 2955968512 | bytes 14876672 | tf_op jit(solution)/shard_map/dot_general | solution.py:141
  395.5 5.9 %all-to-all-start.2 = ((bf16[32,16,4096]{2,1,0:T(8,128)(2,1)}), bf16[32,16,4096]{2,1,0:T(8,128)(2,1)}, u32[]{:S(2)}, u32[]{:S(2)}) async-start(bf16[32,16,4096]{2,1,0:T(8,128)(2,1)} %bitcast.59), calls=%async_computation.2 | async-start | bytes 8388608 | tf_op jit(solution)/shard_map/all_to_all | solution.py:39
  401.5 0.3 all-gather.8.cloned.1.call-start
  401.7 1.2 slice_reduce_fusion
  402.9 3.5 gather_fusion.3
  406.4 0.1 dynamic_slice.10
  406.5 89.5 %all-to-all-done.2 = bf16[32,16,4096]{2,1,0:T(8,128)(2,1)} async-done(((bf16[32,16,4096]{2,1,0:T(8,128)(2,1)}), bf16[32,16,4096]{2,1,0:T(8,128)(2,1)}, u32[]{:S(2)}, u32[]{:S(2)}) %all-to-all-start.2) | async-done | bytes 4194336 | tf_op jit(solution)/shard_map/all_to_all | solution.py:39
  496.0 2.8 convert_reduce_fusion
  498.8 1.7 fusion.21
  500.5 0.9 fusion.49
  501.5 76.5 %all-gather.8.cloned.1.call-done = bf16[512,4096]{1,0:T(8,128)(2,1)} async-done(((bf16[16,4096]{1,0:T(8,128)(2,1)}), bf16[512,4096]{1,0:T(8,128)(2,1)}) %all-gather.8.cloned.1.call-update) | async-done | bytes 4194320 | tf_op jit(solution)/shard_map/all_gather | solution.py:146
  577.9 5.9 gather_fusion.5
  583.8 2.7 broadcast_select_fusion
  (26 shorter events, 0.2 us)
Async XLA Ops:
  6.5 379.8 %copy-start = (bf16[352,4096]{1,0:T(8,128)(2,1)S(1)}, bf16[352,4096]{1,0:T(8,128)(2,1)}, u32[]{:S(2)}) copy-start(bf16[352,4096]{1,0:T(8,128)(2,1)} %param.23) | copy-start | bytes 8650756
  6.5 109.8 %all-gather.4.cloned.1.call-start = ((), (), s32[]{:S(2)}) async-start(), calls=%async_computation.3 | async-start | bytes 8921088 | tf_op jit(solution)/shard_map/all_gather | solution.py:82
  160.2 5.5 copy-start.4
  162.5 3.5 copy-start.1
  169.3 17.6 %all-to-all-start = ((bf16[32,2,4,512]{3,2,1,0:T(4,128)(2,1)}), bf16[32,2,4,512]{3,2,1,0:T(4,128)(2,1)S(1)}, u32[]{:S(2)}, u32[]{:S(2)}) async-start(bf16[32,2,4,512]{3,2,1,0:T(4,128)(2,1)} %bitcast.42), calls=%async_computation | async-start | bytes 524288 | tf_op jit(solution)/shard_map/all_to_all | solution.py:112
  190.5 1.0 copy-start.2
  196.8 100.7 %all-to-all-start.1 = ((bf16[32,16,4096]{2,1,0:T(8,128)(2,1)}), bf16[32,16,4096]{2,1,0:T(8,128)(2,1)}, u32[]{:S(2)}, u32[]{:S(2)}) async-start(bf16[32,16,4096]{2,1,0:T(8,128)(2,1)} %bitcast.58), calls=%async_computation.1 | async-start | bytes 8388608 | tf_op jit(solution)/shard_map/all_to_all | solution.py:39
  201.7 99.8 %copy-start.3 = (f32[4096]{0:T(1024)S(1)}, f32[4096]{0:T(1024)}, u32[]{:S(2)}) copy-start(f32[4096]{0:T(1024)} %param.20) | copy-start | bytes 49156
  201.7 179.0 %all-gather.6.cloned.1.call-start = ((), (), s32[]{:S(2)}) async-start(), calls=%async_computation.4 | async-start | bytes 4325376 | tf_op jit(solution)/shard_map/all_gather | solution.py:136
  395.5 100.5 %all-to-all-start.2 = ((bf16[32,16,4096]{2,1,0:T(8,128)(2,1)}), bf16[32,16,4096]{2,1,0:T(8,128)(2,1)}, u32[]{:S(2)}, u32[]{:S(2)}) async-start(bf16[32,16,4096]{2,1,0:T(8,128)(2,1)} %bitcast.59), calls=%async_computation.2 | async-start | bytes 8388608 | tf_op jit(solution)/shard_map/all_to_all | solution.py:39
  401.5 176.5 %all-gather.8.cloned.1.call-start = ((), (), s32[]{:S(2)}) async-start(), calls=%async_computation.5 | async-start | bytes 4325376 | tf_op jit(solution)/shard_map/all_gather | solution.py:146
Sparse Core Ops, SparseCore 0:
  13.5 102.8 all-gather.3
  303.3 77.3 all-gather.5
  500.7 77.2 all-gather.7
where the time goes:
time: 594 us; the launch traced here: 593 us
  waiting for transfers between devices  449 us (76%)
  other arithmetic  43.2 us (7%)
  local copies, waits for them, and re-layouts  42.8 us (7%)
  matrix products  27.6 us (5%)
  starting transfers between devices  16.9 us (3%)
  between operations  13.4 us (2%)
    all_to_all x2, waiting for transfers between devices, reduce_scatter_rows(): lax.all_to_all(partial.reshape(ctx_size, rows // ctx_size, width), 'ctx',...  185 us
    all_gather x1, waiting for transfers between devices, body(): all_packed = lax.all_gather(packed, 'ctx', axis=0, tiled=True)  103 us
    all_gather x1, waiting for transfers between devices, body(): normed_ffn = lax.all_gather(normed_own, 'ctx', axis=0, tiled=True)  77.5 us
    all_gather x1, waiting for transfers between devices, body(): final_all = lax.all_gather(final_own, 'ctx', axis=0, tiled=True)  76.5 us
    gather x3, other arithmetic, body(): flat_row = source * MOST + rank_ids - run_starts[source]  19.8 us
    gather x1, local copies, waits for them, and re-layouts, body(): picked_rows = all_rows[flat_row]  13 us
  transfers between devices with their start and end apart: 6, of which 6 were waited for; matrix products, arithmetic and copies ran while one was open for 2% of the time, Pallas kernels for 0%

commit v1 on v0

--- a/solution.py
+++ b/solution.py
@@ -133,7 +133,11 @@
     )
     mixed_own = own_rows + attn_own
     normed_own = rms_scale(mixed_own, ffn_gain).astype(jnp.bfloat16)
-    normed_ffn = lax.all_gather(normed_own, "ctx", axis=0, tiled=True)
+    size = lax.axis_size("ctx")
+    repeats = [size if d == 0 else 1 for d in range(normed_own.ndim)]
+    normed_ffn = lax.all_to_all(
+        jnp.tile(normed_own, repeats), "ctx", split_axis=0, concat_axis=0, tiled=True
+    )
     gate_proj = jnp.dot(normed_ffn, gate_weight, preferred_element_type=jnp.float32)
     up_proj = jnp.dot(normed_ffn, up_weight, preferred_element_type=jnp.float32)
     hidden = (jax.nn.silu(gate_proj) * up_proj).astype(jnp.bfloat16)

time: 594 us -> 618 us (1.040)
  blocking collectives: 0 us -> 100 us
  waiting for transfers between devices: 449 us -> 375 us
    all_to_all x0 -> x1, blocking collectives: none -> 100 us  [body(): lax.all_to_all(jnp.tile(normed_own, repeats), 'ctx', split_axis=0, concat...]
    all_gather x1 -> x0, waiting for transfers between devices: 77.5 us -> none  [body(): normed_ffn = lax.all_gather(normed_own, 'ctx', axis=0, tiled=True)]
  transfers between devices with their start and end apart: 6 -> 5, of which waited for: 6 -> 5; matrix products, arithmetic and copies ran while one was open for 2% -> 2% of each run, Pallas kernels for 0% -> 0%
where the time goes in v1:
time: 618 us; the launch traced here: 617 us
  waiting for transfers between devices  375 us (61%)
  blocking collectives  100 us (16%)
  local copies, waits for them, and re-layouts  45.3 us (7%)
  other arithmetic  42.5 us (7%)
  matrix products  24.6 us (4%)
  starting transfers between devices  16.1 us (3%)
  between operations  13.7 us (2%)
    all_to_all x2, waiting for transfers between devices, reduce_scatter_rows(): lax.all_to_all(partial.reshape(ctx_size, rows // ctx_size, width), 'ctx',...  187 us
    all_gather x1, waiting for transfers between devices, body(): all_packed = lax.all_gather(packed, 'ctx', axis=0, tiled=True)  103 us
    all_to_all x1, blocking collectives, body(): lax.all_to_all(jnp.tile(normed_own, repeats), 'ctx', split_axis=0, concat...  100 us
    all_gather x1, waiting for transfers between devices, body(): final_all = lax.all_gather(final_own, 'ctx', axis=0, tiled=True)  77.3 us
    gather x3, other arithmetic, body(): flat_row = source * MOST + rank_ids - run_starts[source]  19.8 us
    gather x1, local copies, waits for them, and re-layouts, body(): picked_rows = all_rows[flat_row]  13 us
  transfers between devices with their start and end apart: 5, of which 5 were waited for; matrix products, arithmetic and copies ran while one was open for 2% of the time, Pallas kernels for 0%

profile of v1, /device:TPU:2, one launch (start us, length us, event | category | flops | bytes accessed | tf_op | source)
XLA Modules:
  0.0 616.9 jit_solution(11148454472538763149)
XLA Ops:
  6.5 0.8 broadcast_compare_fusion
  7.4 0.8 copy.22
  8.2 0.2 reduce-window.13
  8.3 0.1 add_reduce_fusion
  8.5 0.1 fusion.55
  8.6 0.1 select_reduce_fusion
  8.7 1.4 gather_fusion.1
  10.1 2.3 gather_fusion
  12.4 0.1 broadcast_select_fusion.1
  12.5 0.1 select_select_fusion
  12.6 0.7 pad_maximum_fusion
  13.4 102.9 %all-gather.3.cloned.1.call-done = bf16[1024,4224]{1,0:T(8,128)(2,1)} async-done(((bf16[32,4224]{1,0:T(8,128)(2,1)}), bf16[1024,4224]{1,0:T(8,128)(2,1)}) %all-gather.3.cloned.1.call-update) | async-done | bytes 8650768 | tf_op jit(solution)/shard_map/all_gather | solution.py:82
  116.3 1.3 convert_reduce_fusion.2
  117.6 0.1 reshape.508
  117.7 0.1 reduce_sum.78
  117.8 0.1 copy.23
  117.9 0.1 reduce-window.14
  118.0 0.1 reduce.2
  118.1 0.1 convert_reduce_fusion.4
  118.2 0.7 fusion.77
  118.9 0.7 fusion.76
  119.6 4.4 compare_select_fusion.5
  124.0 0.2 compare_reduce_fusion.24
  124.1 15.2 %select_select_fusion.1 = s32[512]{0:T(512)S(1)} fusion(pred[512]{0:T(512)(128)(4,1)S(1)} %get-tuple-element.31, pred[512]{0:T(512)(128)(4,1)S(1)} %get-tuple-element.30, pred[512]{0:T(512)(128)(4,1)S(1)} %get-tuple-element.29, pred[512]{0:T(512)(128)(4,1)S(1)} %get-tuple-element.28, pred[512]{0:T(512)(128)(4,1)S(1)} %get-tuple-element.27, ...), kind=kLoop, calls=%fused_computation.170 | loop fusion | flops 12800 | bytes 16996 | tf_op jit(solution)/shard_map/gather | solution.py:97
  139.4 7.7 %slice.81 = bf16[1024,4096]{1,0:T(8,128)(2,1)} slice(bf16[1024,4224]{1,0:T(8,128)(2,1)} %all-gather.3.cloned.1.call-done), slice={[0:1024], [0:4096]} | slice | bytes 16777216 | tf_op jit(solution)/shard_map/slice | solution.py:83
  147.2 13.0 %gather_fusion.2 = bf16[512,4096]{1,0:T(8,128)(2,1)} fusion(bf16[1024,4096]{1,0:T(8,128)(2,1)} %slice.81, s32[1024]{0:T(1024)S(1)} %pad_clamp_fusion.1), kind=kCustom, calls=%fused_computation.2 | custom fusion | bytes 8390656 | tf_op jit(solution)/shard_map/gather | solution.py:98
  160.2 2.3 gather_fusion.4
  162.5 3.2 fusion
  165.8 0.2 copy-done.1
  165.9 2.5 fusion.9
  168.5 0.8 broadcast_in_dim.126
  169.3 5.8 all-to-all-start
  175.1 4.8 fusion.7
  179.9 6.9 %all-to-all-done = bf16[32,2,4,512]{3,2,1,0:T(4,128)(2,1)S(1)} async-done(((bf16[32,2,4,512]{3,2,1,0:T(4,128)(2,1)}), bf16[32,2,4,512]{3,2,1,0:T(4,128)(2,1)S(1)}, u32[]{:S(2)}, u32[]{:S(2)}) %all-to-all-start) | async-done | bytes 262176 | tf_op jit(solution)/shard_map/all_to_all | solution.py:112
  186.8 0.7 slice_convert_fusion
  187.5 0.1 reshape.510
  187.6 0.9 reshape_squeeze.4
  188.6 1.6 fusion.35
  190.1 0.4 fusion.78
  190.5 1.0 copy-done.3
  191.5 0.2 fusion.12
  191.7 5.1 convolution_convert_fusion
  196.8 4.9 all-to-all-start.1
  201.7 95.8 %all-to-all-done.1 = bf16[32,16,4096]{2,1,0:T(8,128)(2,1)} async-done(((bf16[32,16,4096]{2,1,0:T(8,128)(2,1)}), bf16[32,16,4096]{2,1,0:T(8,128)(2,1)}, u32[]{:S(2)}, u32[]{:S(2)}) %all-to-all-start.1) | async-done | bytes 4194336 | tf_op jit(solution)/shard_map/all_to_all | solution.py:39
  297.5 2.9 convert_reduce_fusion.1
  300.4 1.1 multiply_reduce_fusion
  301.5 1.0 multiply_convert_fusion
  302.5 0.5 tile.2
  303.0 100.2 %all_to_all.24 = bf16[32,16,4096]{2,1,0:T(8,128)(2,1)S(1)} all-to-all(bf16[32,16,4096]{2,1,0:T(8,128)(2,1)S(1)} %tile.2), channel_id=1, replica_groups=mesh['dp'=8,'ctx'=32] {'ctx'}, dimensions={0} | all-to-all | bytes 8388608 | tf_op jit(solution)/shard_map/all_to_all | solution.py:138
  403.3 1.9 copy-done.2
  405.2 2.6 fusion.79
  407.8 9.2 %convolution_convert_fusion.1 = bf16[512,4096]{1,0:T(8,128)(2,1)} fusion(bf16[352,4096]{1,0:T(8,128)(2,1)S(1)} %copy-done, bf16[512,4096]{1,0:T(8,128)(2,1)} %bitcast.62, bf16[4096,352]{0,1:T(8,128)(2,1)} %param.22, f32[512,352]{0,1:T(8,128)} %fusion.79), kind=kOutput, calls=%fused_computation.14 | convolution fusion | flops 2955968512 | bytes 14876672 | tf_op jit(solution)/shard_map/dot_general | solution.py:145
  416.9 5.2 all-to-all-start.3
  422.1 0.3 all-gather.5.cloned.1.call-start
  422.4 1.2 slice_reduce_fusion
  423.6 3.5 gather_fusion.3
  427.1 0.1 dynamic_slice.10
  427.2 91.5 %all-to-all-done.3 = bf16[32,16,4096]{2,1,0:T(8,128)(2,1)} async-done(((bf16[32,16,4096]{2,1,0:T(8,128)(2,1)}), bf16[32,16,4096]{2,1,0:T(8,128)(2,1)}, u32[]{:S(2)}, u32[]{:S(2)}) %all-to-all-start.3) | async-done | bytes 4194336 | tf_op jit(solution)/shard_map/all_to_all | solution.py:39
  518.6 2.8 convert_reduce_fusion
  521.5 1.7 fusion.21
  523.2 0.9 fusion.49
  524.1 77.3 %all-gather.5.cloned.1.call-done = bf16[512,4096]{1,0:T(8,128)(2,1)} async-done(((bf16[16,4096]{1,0:T(8,128)(2,1)}), bf16[512,4096]{1,0:T(8,128)(2,1)}) %all-gather.5.cloned.1.call-update) | async-done | bytes 4194320 | tf_op jit(solution)/shard_map/all_gather | solution.py:150
  601.5 5.9 gather_fusion.5
  607.4 2.7 broadcast_select_fusion
  (29 shorter events, 0.2 us)
Async XLA Ops:
  6.5 401.2 %copy-start = (bf16[352,4096]{1,0:T(8,128)(2,1)S(1)}, bf16[352,4096]{1,0:T(8,128)(2,1)}, u32[]{:S(2)}) copy-start(bf16[352,4096]{1,0:T(8,128)(2,1)} %param.23) | copy-start | bytes 8650756
  6.5 109.8 %all-gather.3.cloned.1.call-start = ((), (), s32[]{:S(2)}) async-start(), calls=%async_computation.4 | async-start | bytes 8921088 | tf_op jit(solution)/shard_map/all_gather | solution.py:82
  160.2 5.5 copy-start.6
  162.5 3.5 copy-start.1
  169.3 17.6 %all-to-all-start = ((bf16[32,2,4,512]{3,2,1,0:T(4,128)(2,1)}), bf16[32,2,4,512]{3,2,1,0:T(4,128)(2,1)S(1)}, u32[]{:S(2)}, u32[]{:S(2)}) async-start(bf16[32,2,4,512]{3,2,1,0:T(4,128)(2,1)} %bitcast.42), calls=%async_computation | async-start | bytes 524288 | tf_op jit(solution)/shard_map/all_to_all | solution.py:112
  190.5 1.0 copy-start.3
  196.8 100.7 %all-to-all-start.1 = ((bf16[32,16,4096]{2,1,0:T(8,128)(2,1)}), bf16[32,16,4096]{2,1,0:T(8,128)(2,1)}, u32[]{:S(2)}, u32[]{:S(2)}) async-start(bf16[32,16,4096]{2,1,0:T(8,128)(2,1)} %bitcast.59), calls=%async_computation.1 | async-start | bytes 8388608 | tf_op jit(solution)/shard_map/all_to_all | solution.py:39
  201.7 99.8 %copy-start.4 = (f32[4096]{0:T(1024)S(1)}, f32[4096]{0:T(1024)}, u32[]{:S(2)}) copy-start(f32[4096]{0:T(1024)} %param.20) | copy-start | bytes 49156
  303.0 102.2 %copy-start.5 = (bf16[4096,352]{0,1:T(8,128)(2,1)S(1)}, bf16[4096,352]{0,1:T(8,128)(2,1)}, u32[]{:S(2)}) copy-start(bf16[4096,352]{0,1:T(8,128)(2,1)} %param.21) | copy-start | bytes 8650756
  403.2 1.9 copy-start.2
  416.9 101.7 %all-to-all-start.3 = ((bf16[32,16,4096]{2,1,0:T(8,128)(2,1)}), bf16[32,16,4096]{2,1,0:T(8,128)(2,1)}, u32[]{:S(2)}, u32[]{:S(2)}) async-start(bf16[32,16,4096]{2,1,0:T(8,128)(2,1)} %bitcast.60), calls=%async_computation.3 | async-start | bytes 8388608 | tf_op jit(solution)/shard_map/all_to_all | solution.py:39
  422.1 179.3 %all-gather.5.cloned.1.call-start = ((), (), s32[]{:S(2)}) async-start(), calls=%async_computation.5 | async-start | bytes 4325376 | tf_op jit(solution)/shard_map/all_gather | solution.py:150
Sparse Core Ops, SparseCore 0:
  13.5 102.8 all-gather.2
  523.3 78.1 all-gather.4
